TPU v7x, 32 devices: a whole 2x2x4 slice. The times are simulated.
32 devices in a mesh: groups: 2 (over y), blk: 8 (over z, x), mp: 2 (over core).
Axes of the slice: x: 2, y: 2, z: 4, core: 2. Of those that a mesh axis runs over, the one named last changes fastest.
Arguments:
- probe_vectors: bfloat16 [12, 8, 32, 3584], P('groups', 'blk', None, 'mp'), parts along dimension 0, may hold values from -12 to 12
- unsettled_lookups: bfloat16 [12, 8, 32, 512], P('groups', 'blk', None, 'mp'), parts along dimension 0, may hold values from -6 to 6
- unsettled_payloads: bfloat16 [12, 8, 32, 512], P('groups', 'blk', None, 'mp'), parts along dimension 0, may hold values from -6 to 6
- uncover_ordering: int32 [12, 8, 32], P('groups', 'blk'), parts along dimension 0, may hold values from 0 to 31, each once within a row
- rounds_finished: int32 [12, 8], P('groups', 'blk'), parts along dimension 0, may hold values from 0 to 7
- random_entry_choice: int32 [12, 8, 32], P('groups', 'blk'), parts along dimension 0, may hold values from 0 to 63
- noise_token_keys: bfloat16 [64, 512], P(None, 'mp'), may hold values from -6 to 6
- noise_token_values: bfloat16 [64, 512], P(None, 'mp'), may hold values from -6 to 6
- prefix_key_cache: bfloat16 [2, 8, 32, 512], P('groups', 'blk', None, 'mp'), parts along dimension 0, may hold values from -6 to 6
- prefix_value_cache: bfloat16 [2, 8, 32, 512], P('groups', 'blk', None, 'mp'), parts along dimension 0, may hold values from -6 to 6
- completed_keys: bfloat16 [16, 32, 512], P(('groups', 'blk'), None, 'mp'), parts along dimension 0, may hold values from -6 to 6
- completed_values: bfloat16 [16, 32, 512], P(('groups', 'blk'), None, 'mp'), parts along dimension 0, may hold values from -6 to 6
- committing_index: int32 [2], P('groups'), parts along dimension 0, may hold values from 0 to 7, as said below
Outputs:
- attended: bfloat16 [12, 8, 32, 3584], P('groups', 'blk', None, 'mp'), parts along dimension 0
There are 2 independent parts, one for each index of `groups`. A program takes and returns all parts, laid end to end along the dimension named above; an argument that names none is the same for every part. Nothing has to cross between parts.
Inputs may be any that keep to these rules, and one draw needn't show every extreme that they name: `committing_index`: an index of blk; in every odd part it is the last index, 7.
All inputs are finite; a program needn't handle non-finite values.
Results may differ from a plain program's by a relative error of at most 0.005.
Values may be sent and summed in bfloat16 or wider, within the bound.
No kernel may reach another device: no remote copies, remote signals or barrier semaphores. Data moves between devices by JAX's collectives and lax.ppermute only.
A program may use at most 128 MiB of HBM per device.

v0:
```python
import math

import jax
import jax.numpy as jnp
from jax import lax
from jax.experimental import pallas as pl
from jax.experimental.pallas import tpu as pltpu
from jax.sharding import PartitionSpec as P


QUERY_GROUPS = 28
MEMORY_GROUPS = 4
FEATURE_DIM = 128
UNMASK = 4
GROUP = QUERY_GROUPS // MEMORY_GROUPS
RATE = FEATURE_DIM ** (-0.5) * math.log2(math.e)

SMALL = 4


def turn_of():
    return (lax.axis_index("blk") == lax.axis_size("blk") - 1).astype(jnp.int32)


def column(row):
    n = row.shape[1]
    here = lax.broadcasted_iota(jnp.int32, (n, n), 0)
    there = lax.broadcasted_iota(jnp.int32, (n, n), 1)
    return jnp.sum(jnp.where(here == there, row, 0), axis=1, keepdims=True)


def blend_kernel(*refs):
    count = (len(refs) - 3) // 2
    sources, (own, keep), places = refs[:count], refs[count : count + 2], refs[count + 2 : -1]
    sems = refs[-1]
    copies = [
        pltpu.make_async_copy(src, dst, sems.at[i])
        for i, (src, dst) in enumerate(zip(sources, places))
    ]
    for copy in copies:
        copy.start()
    for copy in copies:
        copy.wait()
    rounds, order, choice, table_k, table_v, open_k, open_v = places
    slots, block = open_k.shape[0], open_k.shape[2]
    nrows = table_k.shape[0]
    turn = turn_of()
    masks, hots = [], []
    for s in range(slots):
        mask = jnp.where(order[s] >= UNMASK * rounds[:, s : s + 1], 1, 0)
        keep[s] = jnp.concatenate([mask.astype(jnp.float32)] * (lanes(block) // block), axis=1)
        masks.append(column(mask) > 0)
        picked = column(choice[s])
        hots.append(
            jnp.where(picked == lax.broadcasted_iota(jnp.int32, (block, nrows), 1), 1.0, 0.0)
        )
    onehot = jnp.concatenate(hots, axis=0).astype(jnp.bfloat16)
    for i, (table, opened) in enumerate(((table_k, open_k), (table_v, open_v))):
        noise = jnp.dot(onehot, table[...], preferred_element_type=jnp.float32)
        for s in range(slots):
            mixed = jnp.where(
                masks[s], noise[s * block : (s + 1) * block], opened[s, 0].astype(jnp.float32)
            )
            own[lax.rem(s + turn, slots), i] = mixed.astype(jnp.bfloat16)


def lanes(block):
    return -(-GROUP * block // FEATURE_DIM) * FEATURE_DIM


def scores(query, slot, head, keys):
    first = head * GROUP
    order = [first + g % GROUP for g in range(lanes(query.shape[1]) // query.shape[1])]
    q = jnp.concatenate(
        [query[slot, :, g * FEATURE_DIM : (g + 1) * FEATURE_DIM] for g in order], axis=0
    )
    return lax.dot_general(
        keys, q, (((1,), (1,)), ((), ())), preferred_element_type=jnp.float32
    )


def gathered(values, weight):
    ones = jnp.ones((16, values.shape[0]), values.dtype)
    lhs = jnp.concatenate([jnp.transpose(values), ones], axis=0)
    got = jnp.dot(lhs, weight, preferred_element_type=jnp.float32)
    return got[:FEATURE_DIM], got[FEATURE_DIM : FEATURE_DIM + 1]


def staggered(slots, heads, blocks, stages):
    def run(tasks):
        held = {}
        for step in range(-(-len(tasks) // 3) + len(stages) - 1):
            for k, stage in enumerate(stages):
                for i in range(3 * (step - k), 3 * (step - k) + 3):
                    if 0 <= i < len(tasks):
                        held[i] = stage(*tasks[i], *held.get(i, ()))

    if blocks <= SMALL:
        run([(s, h) for s in range(slots) for h in range(heads)])
    else:
        pl.loop(0, slots)(lambda s: run([(s, h) for h in range(heads)]))


def grant(blocks):
    return pltpu.CompilerParams(vmem_limit_bytes=20 << 20) if blocks <= SMALL else None


def columns(head):
    return slice(head * FEATURE_DIM, (head + 1) * FEATURE_DIM)


def first_kernel(took, query, outer, inner, side, own, tops, totals, sums, mine):
    slots, _, _, width = own.shape
    last = side.shape[0]
    mine[...] = jnp.full(mine.shape, took[0], jnp.int32)

    def stack(s, h, i):
        at = lax.rem(s + turn_of(), slots)
        parts = [a[b, i, :, columns(h)] for a in (outer, inner, side) for b in range(last)]
        return jnp.concatenate(parts + [own[at, i, :, columns(h)]], axis=0)

    def score(s, h):
        return (scores(query, s, h, stack(s, h, 0)),)

    def peak(s, h, score):
        top = jnp.max(score, axis=0, keepdims=True)
        tops[s, h] = top
        return score, top

    def weigh(s, h, score, top):
        weight = jnp.exp2((score - top) * RATE)
        return (weight.astype(jnp.bfloat16),)

    def gather(s, h, weight):
        sums[s, h], totals[s, h] = gathered(stack(s, h, 1), weight)

    staggered(slots, width // FEATURE_DIM, last, (score, peak, weigh, gather))


def last_kernel(query, inner, far, prev, keep, tops, totals, sums, mine, out, made, pick, sems):
    slots, _, block, width = prev.shape
    heads = width // FEATURE_DIM
    last = far.shape[0] - 1
    take = mine[:1, :] > 0
    for i in range(2):
        for h in range(heads):
            pick[i, :, columns(h)] = jnp.where(
                take, inner[last, i, :, columns(h)], far[last, i, :, columns(h)]
            )

    def copy_of(s):
        return pltpu.make_async_copy(made.at[s], out.at[s], sems.at[s])

    def stack(s, h, i):
        parts = [far[b, i, :, columns(h)] for b in range(last)]
        parts.append(pick[i, :, columns(h)])
        parts.append(prev[s, i, :, columns(h)])
        return jnp.concatenate(parts, axis=0)

    def score(s, h):
        return (scores(query, s, h, stack(s, h, 0)),)

    def peak(s, h, score):
        before = tops[s, h]
        top = jnp.maximum(before, jnp.max(score, axis=0, keepdims=True))
        return score, top, jnp.exp2((before - top) * RATE)

    def weigh(s, h, score, top, factor):
        weight = jnp.exp2((score - top) * RATE)
        return weight.astype(jnp.bfloat16), factor

    def gather(s, h, weight, factor):
        return *gathered(stack(s, h, 1), weight), factor

    def finish(s, h, context, total, factor):
        total = totals[s, h] * factor + total
        share = jnp.where(keep[s] > 0, 1.0 / total, 0.0)
        old = factor * share
        context = sums[s, h] * old + context * share
        context = jnp.transpose(context.astype(jnp.bfloat16))
        for g in range(GROUP):
            at = (h * GROUP + g) * FEATURE_DIM
            made[s, :, at : at + FEATURE_DIM] = context[g * block : (g + 1) * block]
        if h == heads - 1:
            copy_of(s).start()

    staggered(slots, heads, last, (score, peak, weigh, gather, finish))
    staggered(slots, 1, last, (lambda s, h: copy_of(s).wait(),))


def swap(block, axis, bit):
    size = lax.axis_size(axis)
    return lax.ppermute(block, axis, [(i, i ^ bit) for i in range(size)])


def on_device(
    probe_vectors,
    unsettled_lookups,
    unsettled_payloads,
    uncover_ordering,
    rounds_finished,
    random_entry_choice,
    noise_token_keys,
    noise_token_values,
    prefix_key_cache,
    prefix_value_cache,
    completed_keys,
    completed_values,
    committing_index,
):
    slots, block = probe_vectors.shape[0], probe_vectors.shape[2]
    wide = probe_vectors.shape[3]
    width = noise_token_keys.shape[1]
    size = lax.axis_size("blk")
    me = lax.axis_index("blk")
    owner = committing_index[0]
    rounds = rounds_finished.reshape(1, slots)

    vm = pl.BlockSpec(memory_space=pltpu.VMEM)
    sm = pl.BlockSpec(memory_space=pltpu.SMEM)

    packed = jnp.stack(
        [
            a.reshape(block, width)
            for a in (prefix_key_cache, prefix_value_cache, completed_keys, completed_values)
        ]
    ).reshape(2, 2, block, width)

    sources = (
        rounds,
        uncover_ordering,
        random_entry_choice,
        noise_token_keys,
        noise_token_values,
        unsettled_lookups,
        unsettled_payloads,
    )
    own, keep = pl.pallas_call(
        blend_kernel,
        out_shape=[
            pltpu.VMEM((slots, 2, block, width), jnp.bfloat16),
            pltpu.VMEM((slots, 1, lanes(block)), jnp.float32),
        ],
        in_specs=[pl.BlockSpec(memory_space=pltpu.HBM)] * len(sources),
        out_specs=[vm] * 2,
        scratch_shapes=[pltpu.VMEM(a.shape, a.dtype) for a in sources]
        + [pltpu.SemaphoreType.DMA((len(sources),))],
        compiler_params=pltpu.CompilerParams(vmem_limit_bytes=4 << 20),
        name="blend",
    )(*(pltpu.with_memory_space_constraint(a, pltpu.HBM) for a in sources))
    prev = lax.ppermute(own, "blk", [(i, (i + 1) % size) for i in range(size)])
    bits = [1 << b for b in reversed(range(size.bit_length() - 1))]
    bits = bits[-1:] + bits[:-1]
    for hop, bit in enumerate(bits):
        packed = lax.optimization_barrier(packed)
        if hop == len(bits) - 2:
            outer = packed
            side = swap(outer[:-1], "blk", bits[-1])
        got = swap(packed, "blk", bit)
        same = (owner & bit) == (me & bit)
        if hop < len(bits) - 1:
            pick = jnp.where(same, packed[-1:], got[-1:])
            known = [] if hop == len(bits) - 2 else [packed[:-1]]
            packed = jnp.concatenate(known + [got[:-1], pick], axis=0)

    took = same.astype(jnp.int32).reshape(1)
    heads = width // FEATURE_DIM
    query = probe_vectors.reshape(slots, block, wide)
    shapes = [(slots, heads, n, lanes(block)) for n in (1, 1, FEATURE_DIM)]
    shapes = [jax.ShapeDtypeStruct(a, jnp.float32) for a in shapes]
    shapes.append(jax.ShapeDtypeStruct((8, FEATURE_DIM), jnp.int32))
    state = pl.pallas_call(
        first_kernel,
        out_shape=shapes,
        in_specs=[sm] + [vm] * 5,
        out_specs=[vm] * len(shapes),
        compiler_params=grant(size // 4),
        name="early",
    )(took, query, outer, packed, side, own)
    out = pl.pallas_call(
        last_kernel,
        out_shape=jax.ShapeDtypeStruct((slots, block, wide), jnp.bfloat16),
        in_specs=[vm] * (5 + len(shapes)),
        out_specs=pl.BlockSpec(memory_space=pl.ANY),
        scratch_shapes=[
            pltpu.VMEM((slots, block, wide), jnp.bfloat16),
            pltpu.VMEM((2, block, width), jnp.bfloat16),
            pltpu.SemaphoreType.DMA((slots,)),
        ],
        compiler_params=grant(size // 4),
        name="late",
    )(query, packed, got, prev, keep, *state)
    return out.reshape(slots, 1, block, wide)


def solution(mesh):
    placed = (
        P("groups", "blk", None, "mp"),
        P("groups", "blk", None, "mp"),
        P("groups", "blk", None, "mp"),
        P("groups", "blk", None),
        P("groups", "blk"),
        P("groups", "blk", None),
        P(None, "mp"),
        P(None, "mp"),
        P("groups", "blk", None, "mp"),
        P("groups", "blk", None, "mp"),
        P(("groups", "blk"), None, "mp"),
        P(("groups", "blk"), None, "mp"),
        P("groups"),
    )

    return jax.shard_map(
        on_device,
        mesh=mesh,
        in_specs=placed,
        out_specs=P("groups", "blk", None, "mp"),
        check_vma=False,
    )
```

profile of v0, /device:TPU:0, one launch (start us, length us, event | category | flops | bytes accessed | tf_op | source)
XLA Modules:
  0.0 22.3 jit_solution(6249417255635885878)
XLA Ops:
  0.0 0.0 copy-start
  0.0 0.8 %pad_maximum_fusion.2 = bf16[4,32,256]{2,1,0:T(8,128)(2,1)S(1)} fusion(bf16[1,32,256]{2,1,0:T(8,128)(2,1)} %param.24, bf16[1,32,256]{2,1,0:T(8,128)(2,1)} %param.23, bf16[1,32,256]{2,1,0:T(8,128)(2,1)} %bitcast.16, bf16[1,32,256]{2,1,0:T(8,128)(2,1)} %bitcast.17), kind=kLoop, calls=%fused_computation.2 | loop fusion | flops 98304 | bytes 131072 | tf_op jit(solution)/shard_map/stack | solution.py:222
  0.8 3.0 %collective-permute-start = (bf16[2,2,32,256]{3,2,1,0:T(8,128)(2,1)S(1)}, bf16[2,2,32,256]{3,2,1,0:T(8,128)(2,1)S(1)}, u32[]{:S(2)}, u32[]{:S(2)}) collective-permute-start(bf16[2,2,32,256]{3,2,1,0:T(8,128)(2,1)S(1)} %bitcast.14), channel_id=1, source_target_pairs={{0,2},{2,0},{4,6},{6,4},{8,10},{10,8},{12,14},{14,12},{1,3},{3,1},... | collective-permute-start | bytes 196616 | tf_op jit(solution)/shard_map/ppermute | solution.py:193
  4.5 1.6 %collective-permute-done = bf16[2,2,32,256]{3,2,1,0:T(8,128)(2,1)S(1)} collective-permute-done((bf16[2,2,32,256]{3,2,1,0:T(8,128)(2,1)S(1)}, bf16[2,2,32,256]{3,2,1,0:T(8,128)(2,1)S(1)}, u32[]{:S(2)}, u32[]{:S(2)}) %collective-permute-start) | collective-permute-done | bytes 65568 | tf_op jit(solution)/shard_map/ppermute | solution.py:193
  6.2 3.2 %collective-permute-start.1 = (bf16[3,2,32,256]{3,2,1,0:T(8,128)(2,1)S(1)}, bf16[3,2,32,256]{3,2,1,0:T(8,128)(2,1)S(1)}, u32[]{:S(2)}, u32[]{:S(2)}) collective-permute-start(bf16[3,2,32,256]{3,2,1,0:T(8,128)(2,1)S(1)} %pad_maximum_fusion.outer), channel_id=1, source_target_pairs={{0,8},{2,10},{4,12},{6,14},{8,0},{10,2},{12,4},{14,6},{1,9},{3,11}... | collective-permute-start | bytes 294920 | tf_op jit(solution)/shard_map/ppermute | solution.py:193
  9.3 1.7 %blend.1 = (bf16[6,2,32,256]{3,2,1,0:T(8,128)(2,1)S(1)}, f32[6,1,256]{2,1,0:T(1,128)S(1)}) custom-call(s32[1,6]{1,0:T(1,128)} %bitcast.18, s32[6,1,32]{2,1,0:T(1,128)} %refs_1_.1, s32[6,1,32]{2,1,0:T(1,128)} %refs_2_.1, bf16[64,256]{1,0:T(8,128)(2,1)} %refs_3_.1, bf16[64,256]{1,0:T(8,128)(2,1)} %refs_4_.1, bf16[6,1,32,256]{3,2,1,0:T(8,128)(2,1)} %refs_5_.1, ...), custom_call_target="tpu_custom_call" | custom-call | tf_op jit(solution)/shard_map/blend/pallas_call | solution.py:238
  11.0 1.5 %collective-permute-start.3 = (bf16[6,2,32,256]{3,2,1,0:T(8,128)(2,1)S(1)}, bf16[6,2,32,256]{3,2,1,0:T(8,128)(2,1)S(1)}, u32[]{:S(2)}, u32[]{:S(2)}) collective-permute-start(bf16[6,2,32,256]{3,2,1,0:T(8,128)(2,1)S(1)} %get-tuple-element.11.own), channel_id=1, source_target_pairs={{0,2},{2,4},{4,6},{6,8},{8,10},{10,12},{12,14},{14,0},{1,3},{3,5},... | collective-permute-start | bytes 589832 | tf_op jit(solution)/shard_map/ppermute | solution.py:251
  12.6 0.0 collective-permute-done.1
  12.6 1.6 %collective-permute-start.2 = (bf16[3,2,32,256]{3,2,1,0:T(8,128)(2,1)S(1)}, bf16[3,2,32,256]{3,2,1,0:T(8,128)(2,1)S(1)}, u32[]{:S(2)}, u32[]{:S(2)}) collective-permute-start(bf16[3,2,32,256]{3,2,1,0:T(8,128)(2,1)S(1)} %pad_maximum_fusion.1.inner), channel_id=1, source_target_pairs={{0,4},{2,6},{4,0},{6,2},{8,12},{10,14},{12,8},{14,10},{1,5},{3,7},... | collective-permute-start | bytes 294920 | tf_op jit(solution)/shard_map/ppermute | solution.py:193
  14.3 0.5 %collective-permute-start.4 = (bf16[2,2,32,256]{3,2,1,0:T(8,128)(2,1)S(1)}, bf16[2,2,32,256]{3,2,1,0:T(8,128)(2,1)S(1)}, u32[]{:S(2)}, u32[]{:S(2)}) collective-permute-start(bf16[2,2,32,256]{3,2,1,0:T(8,128)(2,1)S(1)} %slice.39), channel_id=1, source_target_pairs={{0,4},{2,6},{4,0},{6,2},{8,12},{10,14},{12,8},{14,10},{1,5},{3,7},... | collective-permute-start | bytes 196616 | tf_op jit(solution)/shard_map/ppermute | solution.py:193
  14.7 3.8 %collective-permute-done.4.side = bf16[2,2,32,256]{3,2,1,0:T(8,128)(2,1)S(1)} collective-permute-done((bf16[2,2,32,256]{3,2,1,0:T(8,128)(2,1)S(1)}, bf16[2,2,32,256]{3,2,1,0:T(8,128)(2,1)S(1)}, u32[]{:S(2)}, u32[]{:S(2)}) %collective-permute-start.4) | collective-permute-done | bytes 65568 | tf_op jit(solution)/shard_map/ppermute | solution.py:193
  18.5 0.0 copy-done
  18.5 0.9 %early.1 = (f32[6,2,1,256]{3,2,1,0:T(1,128)S(1)}, f32[6,2,1,256]{3,2,1,0:T(1,128)S(1)}, f32[6,2,128,256]{3,2,1,0:T(8,128)S(1)}, s32[8,128]{1,0:T(8,128)S(1)}) custom-call(s32[1]{0:T(128)} %bitcast.8.took, bf16[6,32,1792]{2,1,0:T(8,128)(2,1)S(1)} %bitcast.12, bf16[3,2,32,256]{3,2,1,0:T(8,128)(2,1)S(1)} %pad_maximum_fusion.outer, ...), custom_call_target="tpu_custom_call" | custom-call | tf_op jit(solution)/shard_map/early/pallas_call | solution.py:272
  19.5 1.3 %collective-permute-done.3.prev = bf16[6,2,32,256]{3,2,1,0:T(8,128)(2,1)S(1)} collective-permute-done((bf16[6,2,32,256]{3,2,1,0:T(8,128)(2,1)S(1)}, bf16[6,2,32,256]{3,2,1,0:T(8,128)(2,1)S(1)}, u32[]{:S(2)}, u32[]{:S(2)}) %collective-permute-start.3) | collective-permute-done | bytes 196640 | tf_op jit(solution)/shard_map/ppermute | solution.py:251
  20.7 0.0 collective-permute-done.2.far
  20.8 1.5 %late.1 = bf16[6,32,1792]{2,1,0:T(8,128)(2,1)} custom-call(bf16[6,32,1792]{2,1,0:T(8,128)(2,1)S(1)} %bitcast.13, bf16[3,2,32,256]{3,2,1,0:T(8,128)(2,1)S(1)} %pad_maximum_fusion.1.inner, bf16[3,2,32,256]{3,2,1,0:T(8,128)(2,1)S(1)} %collective-permute-done.2.far, bf16[6,2,32,256]{3,2,1,0:T(8,128)(2,1)S(1)} %collective-permute-done.3.prev, ...), custom_call_target="tpu_custom_call" | custom-call | tf_op jit(solution)/shard_map/late/pallas_call | solution.py:280
  (6 shorter events, 0.1 us)
Async XLA Ops:
  0.0 18.5 %copy-start = (bf16[6,1,32,1792]{3,2,1,0:T(8,128)(2,1)S(1)}, bf16[6,1,32,1792]{3,2,1,0:T(8,128)(2,1)}, u32[]{:S(2)}) copy-start(bf16[6,1,32,1792]{3,2,1,0:T(8,128)(2,1)} %param.13) | copy-start | bytes 2064388
  0.8 5.3 %collective-permute-start = (bf16[2,2,32,256]{3,2,1,0:T(8,128)(2,1)S(1)}, bf16[2,2,32,256]{3,2,1,0:T(8,128)(2,1)S(1)}, u32[]{:S(2)}, u32[]{:S(2)}) collective-permute-start(bf16[2,2,32,256]{3,2,1,0:T(8,128)(2,1)S(1)} %bitcast.14), channel_id=1, source_target_pairs={{0,2},{2,0},{4,6},{6,4},{8,10},{10,8},{12,14},{14,12},{1,3},{3,1},... | collective-permute-start | bytes 196616 | tf_op jit(solution)/shard_map/ppermute | solution.py:193
  6.2 6.4 %collective-permute-start.1 = (bf16[3,2,32,256]{3,2,1,0:T(8,128)(2,1)S(1)}, bf16[3,2,32,256]{3,2,1,0:T(8,128)(2,1)S(1)}, u32[]{:S(2)}, u32[]{:S(2)}) collective-permute-start(bf16[3,2,32,256]{3,2,1,0:T(8,128)(2,1)S(1)} %pad_maximum_fusion.outer), channel_id=1, source_target_pairs={{0,8},{2,10},{4,12},{6,14},{8,0},{10,2},{12,4},{14,6},{1,9},{3,11}... | collective-permute-start | bytes 294920 | tf_op jit(solution)/shard_map/ppermute | solution.py:193
  11.0 9.7 %collective-permute-start.3 = (bf16[6,2,32,256]{3,2,1,0:T(8,128)(2,1)S(1)}, bf16[6,2,32,256]{3,2,1,0:T(8,128)(2,1)S(1)}, u32[]{:S(2)}, u32[]{:S(2)}) collective-permute-start(bf16[6,2,32,256]{3,2,1,0:T(8,128)(2,1)S(1)} %get-tuple-element.11.own), channel_id=1, source_target_pairs={{0,2},{2,4},{4,6},{6,8},{8,10},{10,12},{12,14},{14,0},{1,3},{3,5},... | collective-permute-start | bytes 589832 | tf_op jit(solution)/shard_map/ppermute | solution.py:251
  12.6 8.1 %collective-permute-start.2 = (bf16[3,2,32,256]{3,2,1,0:T(8,128)(2,1)S(1)}, bf16[3,2,32,256]{3,2,1,0:T(8,128)(2,1)S(1)}, u32[]{:S(2)}, u32[]{:S(2)}) collective-permute-start(bf16[3,2,32,256]{3,2,1,0:T(8,128)(2,1)S(1)} %pad_maximum_fusion.1.inner), channel_id=1, source_target_pairs={{0,4},{2,6},{4,0},{6,2},{8,12},{10,14},{12,8},{14,10},{1,5},{3,7},... | collective-permute-start | bytes 294920 | tf_op jit(solution)/shard_map/ppermute | solution.py:193
  14.3 4.3 %collective-permute-start.4 = (bf16[2,2,32,256]{3,2,1,0:T(8,128)(2,1)S(1)}, bf16[2,2,32,256]{3,2,1,0:T(8,128)(2,1)S(1)}, u32[]{:S(2)}, u32[]{:S(2)}) collective-permute-start(bf16[2,2,32,256]{3,2,1,0:T(8,128)(2,1)S(1)} %slice.39), channel_id=1, source_target_pairs={{0,4},{2,6},{4,0},{6,2},{8,12},{10,14},{12,8},{14,10},{1,5},{3,7},... | collective-permute-start | bytes 196616 | tf_op jit(solution)/shard_map/ppermute | solution.py:193
where the time goes:
time: 22.5 us; the launch traced here: 22.3 us
  starting transfers between devices  9.85 us (44%)
  waiting for transfers between devices  6.69 us (30%)
  Pallas kernels  4.09 us (18%)
  other arithmetic  0.89 us (4%)
  between operations  0.71 us (3%)
    ppermute x4, starting transfers between devices, swap(): return lax.ppermute(block, axis, [(i, i ^ bit) for i in range(size)])  8.31 us
    ppermute x4, waiting for transfers between devices, swap(): return lax.ppermute(block, axis, [(i, i ^ bit) for i in range(size)])  5.41 us
    pallas_call x1, Pallas kernels, on_device(): pl.pallas_call(blend_kernel, out_shape=[pltpu.VMEM((slots, 2, block, widt...  1.68 us
    ppermute x1, starting transfers between devices, on_device(): prev = lax.ppermute(own, 'blk', [(i, (i + 1) % size) for i in range(size)])  1.54 us
    pallas_call x1, Pallas kernels, on_device(): pl.pallas_call(last_kernel, out_shape=jax.ShapeDtypeStruct((slots, block,...  1.5 us
    ppermute x1, waiting for transfers between devices, on_device(): prev = lax.ppermute(own, 'blk', [(i, (i + 1) % size) for i in range(size)])  1.28 us
    pallas_call x1, Pallas kernels, on_device(): pl.pallas_call(first_kernel, out_shape=shapes, in_specs=[sm] + [vm] * 5,...  0.92 us
    another operation x1, other arithmetic, on_device(): jnp.stack([a.reshape(block, width) for a in (prefix_key_cache, prefix_val...  0.84 us
  transfers between devices with their start and end apart: 5, of which 3 were waited for; matrix products, arithmetic and copies ran while one was open for 0% of the time, Pallas kernels for 12%

commit v1 on v0

--- a/solution.py
+++ b/solution.py
@@ -188,9 +188,12 @@
     staggered(slots, 1, last, (lambda s, h: copy_of(s).wait(),))
 
 
-def swap(block, axis, bit):
-    size = lax.axis_size(axis)
-    return lax.ppermute(block, axis, [(i, i ^ bit) for i in range(size)])
+def swap(block, bits):
+    size, cores = lax.axis_size("blk"), lax.axis_size("mp")
+    pairs = [
+        (i * cores + m, (i ^ bits[m % 2]) * cores + m) for i in range(size) for m in range(cores)
+    ]
+    return lax.ppermute(block, ("blk", "mp"), pairs)
 
 
 def on_device(
@@ -251,12 +254,15 @@
     prev = lax.ppermute(own, "blk", [(i, (i + 1) % size) for i in range(size)])
     bits = [1 << b for b in reversed(range(size.bit_length() - 1))]
     bits = bits[-1:] + bits[:-1]
-    for hop, bit in enumerate(bits):
+    other = bits[1:] + bits[:1]
+    odd = lax.axis_index("mp") % 2 == 1
+    for hop, pair in enumerate(zip(bits, other)):
+        bit = jnp.where(odd, pair[1], pair[0])
         packed = lax.optimization_barrier(packed)
         if hop == len(bits) - 2:
             outer = packed
-            side = swap(outer[:-1], "blk", bits[-1])
-        got = swap(packed, "blk", bit)
+            side = swap(outer[:-1], (bits[-1], other[-1]))
+        got = swap(packed, pair)
         same = (owner & bit) == (me & bit)
         if hop < len(bits) - 1:
             pick = jnp.where(same, packed[-1:], got[-1:])

time: 22.5 us -> 21.4 us (0.951)
  waiting for transfers between devices: 6.69 us -> 5.49 us
    ppermute x1, waiting for transfers between devices: 1.28 us -> 0.08 us  [on_device(): prev = lax.ppermute(own, 'blk', [(i, (i + 1) % size) for i in range(size)])]
where the time goes in v1:
time: 21.4 us; the launch traced here: 21.1 us
  starting transfers between devices  9.85 us (46%)
  waiting for transfers between devices  5.49 us (26%)
  Pallas kernels  4.1 us (19%)
  other arithmetic  0.89 us (4%)
  between operations  0.71 us (3%)
    ppermute x4, starting transfers between devices, swap(): return lax.ppermute(block, ('blk', 'mp'), pairs)  8.31 us
    ppermute x4, waiting for transfers between devices, swap(): return lax.ppermute(block, ('blk', 'mp'), pairs)  5.41 us
    pallas_call x1, Pallas kernels, on_device(): pl.pallas_call(blend_kernel, out_shape=[pltpu.VMEM((slots, 2, block, widt...  1.68 us
    ppermute x1, starting transfers between devices, on_device(): prev = lax.ppermute(own, 'blk', [(i, (i + 1) % size) for i in range(size)])  1.54 us
    pallas_call x1, Pallas kernels, on_device(): pl.pallas_call(last_kernel, out_shape=jax.ShapeDtypeStruct((slots, block,...  1.5 us
    pallas_call x1, Pallas kernels, on_device(): pl.pallas_call(first_kernel, out_shape=shapes, in_specs=[sm] + [vm] * 5,...  0.92 us
    another operation x1, other arithmetic, on_device(): jnp.stack([a.reshape(block, width) for a in (prefix_key_cache, prefix_val...  0.84 us
  transfers between devices with their start and end apart: 5, of which 3 were waited for; matrix products, arithmetic and copies ran while one was open for 0% of the time, Pallas kernels for 12%

profile of v1, /device:TPU:0, one launch (start us, length us, event | category | flops | bytes accessed | tf_op | source)
XLA Modules:
  0.0 21.1 jit_solution(3929018612123284841)
XLA Ops:
  0.0 0.0 copy-start
  0.0 0.8 %pad_maximum_fusion.2 = bf16[4,32,256]{2,1,0:T(8,128)(2,1)S(1)} fusion(bf16[1,32,256]{2,1,0:T(8,128)(2,1)} %param.24, bf16[1,32,256]{2,1,0:T(8,128)(2,1)} %param.23, bf16[1,32,256]{2,1,0:T(8,128)(2,1)} %bitcast.17, bf16[1,32,256]{2,1,0:T(8,128)(2,1)} %bitcast.18), kind=kLoop, calls=%fused_computation.2 | loop fusion | flops 98304 | bytes 131072 | tf_op jit(solution)/shard_map/stack | solution.py:225
  0.8 3.0 %collective-permute-start = (bf16[2,2,32,256]{3,2,1,0:T(8,128)(2,1)S(1)}, bf16[2,2,32,256]{3,2,1,0:T(8,128)(2,1)S(1)}, u32[]{:S(2)}, u32[]{:S(2)}) collective-permute-start(bf16[2,2,32,256]{3,2,1,0:T(8,128)(2,1)S(1)} %bitcast.15), channel_id=1, source_target_pairs={{0,2},{1,9},{2,0},{3,11},{4,6},{5,13},{6,4},{7,15},{8,10},{9,1},{1... | collective-permute-start | bytes 196616 | tf_op jit(solution)/shard_map/ppermute | solution.py:196
  4.5 1.6 %collective-permute-done = bf16[2,2,32,256]{3,2,1,0:T(8,128)(2,1)S(1)} collective-permute-done((bf16[2,2,32,256]{3,2,1,0:T(8,128)(2,1)S(1)}, bf16[2,2,32,256]{3,2,1,0:T(8,128)(2,1)S(1)}, u32[]{:S(2)}, u32[]{:S(2)}) %collective-permute-start) | collective-permute-done | bytes 65568 | tf_op jit(solution)/shard_map/ppermute | solution.py:196
  6.2 3.2 %collective-permute-start.1 = (bf16[3,2,32,256]{3,2,1,0:T(8,128)(2,1)S(1)}, bf16[3,2,32,256]{3,2,1,0:T(8,128)(2,1)S(1)}, u32[]{:S(2)}, u32[]{:S(2)}) collective-permute-start(bf16[3,2,32,256]{3,2,1,0:T(8,128)(2,1)S(1)} %pad_maximum_fusion.outer), channel_id=1, source_target_pairs={{0,8},{1,5},{2,10},{3,7},{4,12},{5,1},{6,14},{7,3},{8,0},{9,13},{1... | collective-permute-start | bytes 294920 | tf_op jit(solution)/shard_map/ppermute | solution.py:196
  9.3 1.7 %blend.1 = (bf16[6,2,32,256]{3,2,1,0:T(8,128)(2,1)S(1)}, f32[6,1,256]{2,1,0:T(1,128)S(1)}) custom-call(s32[1,6]{1,0:T(1,128)} %bitcast.19, s32[6,1,32]{2,1,0:T(1,128)} %refs_1_.1, s32[6,1,32]{2,1,0:T(1,128)} %refs_2_.1, bf16[64,256]{1,0:T(8,128)(2,1)} %refs_3_.1, bf16[64,256]{1,0:T(8,128)(2,1)} %refs_4_.1, bf16[6,1,32,256]{3,2,1,0:T(8,128)(2,1)} %refs_5_.1, ...), custom_call_target="tpu_custom_call" | custom-call | tf_op jit(solution)/shard_map/blend/pallas_call | solution.py:241
  11.0 1.5 %collective-permute-start.3 = (bf16[6,2,32,256]{3,2,1,0:T(8,128)(2,1)S(1)}, bf16[6,2,32,256]{3,2,1,0:T(8,128)(2,1)S(1)}, u32[]{:S(2)}, u32[]{:S(2)}) collective-permute-start(bf16[6,2,32,256]{3,2,1,0:T(8,128)(2,1)S(1)} %get-tuple-element.11.own), channel_id=1, source_target_pairs={{0,2},{2,4},{4,6},{6,8},{8,10},{10,12},{12,14},{14,0},{1,3},{3,5},... | collective-permute-start | bytes 589832 | tf_op jit(solution)/shard_map/ppermute | solution.py:254
  12.6 0.0 collective-permute-done.1
  12.6 1.6 %collective-permute-start.2 = (bf16[3,2,32,256]{3,2,1,0:T(8,128)(2,1)S(1)}, bf16[3,2,32,256]{3,2,1,0:T(8,128)(2,1)S(1)}, u32[]{:S(2)}, u32[]{:S(2)}) collective-permute-start(bf16[3,2,32,256]{3,2,1,0:T(8,128)(2,1)S(1)} %pad_maximum_fusion.1.inner), channel_id=1, source_target_pairs={{0,4},{1,3},{2,6},{3,1},{4,0},{5,7},{6,2},{7,5},{8,12},{9,11},{10,... | collective-permute-start | bytes 294920 | tf_op jit(solution)/shard_map/ppermute | solution.py:196
  14.3 0.5 %collective-permute-start.4 = (bf16[2,2,32,256]{3,2,1,0:T(8,128)(2,1)S(1)}, bf16[2,2,32,256]{3,2,1,0:T(8,128)(2,1)S(1)}, u32[]{:S(2)}, u32[]{:S(2)}) collective-permute-start(bf16[2,2,32,256]{3,2,1,0:T(8,128)(2,1)S(1)} %slice.39), channel_id=1, source_target_pairs={{0,4},{1,3},{2,6},{3,1},{4,0},{5,7},{6,2},{7,5},{8,12},{9,11},{10,... | collective-permute-start | bytes 196616 | tf_op jit(solution)/shard_map/ppermute | solution.py:196
  14.7 3.8 %collective-permute-done.4.side = bf16[2,2,32,256]{3,2,1,0:T(8,128)(2,1)S(1)} collective-permute-done((bf16[2,2,32,256]{3,2,1,0:T(8,128)(2,1)S(1)}, bf16[2,2,32,256]{3,2,1,0:T(8,128)(2,1)S(1)}, u32[]{:S(2)}, u32[]{:S(2)}) %collective-permute-start.4) | collective-permute-done | bytes 65568 | tf_op jit(solution)/shard_map/ppermute | solution.py:196
  18.5 0.0 copy-done
  18.5 0.9 %early.1 = (f32[6,2,1,256]{3,2,1,0:T(1,128)S(1)}, f32[6,2,1,256]{3,2,1,0:T(1,128)S(1)}, f32[6,2,128,256]{3,2,1,0:T(8,128)S(1)}, s32[8,128]{1,0:T(8,128)S(1)}) custom-call(s32[1]{0:T(128)} %bitcast.6.took, bf16[6,32,1792]{2,1,0:T(8,128)(2,1)S(1)} %bitcast.13, bf16[3,2,32,256]{3,2,1,0:T(8,128)(2,1)S(1)} %pad_maximum_fusion.outer, ...), custom_call_target="tpu_custom_call" | custom-call | tf_op jit(solution)/shard_map/early/pallas_call | solution.py:278
  19.5 0.1 collective-permute-done.3.prev
  19.6 0.0 collective-permute-done.2.far
  19.6 1.5 %late.1 = bf16[6,32,1792]{2,1,0:T(8,128)(2,1)} custom-call(bf16[6,32,1792]{2,1,0:T(8,128)(2,1)S(1)} %bitcast.14, bf16[3,2,32,256]{3,2,1,0:T(8,128)(2,1)S(1)} %pad_maximum_fusion.1.inner, bf16[3,2,32,256]{3,2,1,0:T(8,128)(2,1)S(1)} %collective-permute-done.2.far, bf16[6,2,32,256]{3,2,1,0:T(8,128)(2,1)S(1)} %collective-permute-done.3.prev, ...), custom_call_target="tpu_custom_call" | custom-call | tf_op jit(solution)/shard_map/late/pallas_call | solution.py:286
  (6 shorter events, 0.1 us)
Async XLA Ops:
  0.0 18.5 %copy-start = (bf16[6,1,32,1792]{3,2,1,0:T(8,128)(2,1)S(1)}, bf16[6,1,32,1792]{3,2,1,0:T(8,128)(2,1)}, u32[]{:S(2)}) copy-start(bf16[6,1,32,1792]{3,2,1,0:T(8,128)(2,1)} %param.13) | copy-start | bytes 2064388
  0.8 5.3 %collective-permute-start = (bf16[2,2,32,256]{3,2,1,0:T(8,128)(2,1)S(1)}, bf16[2,2,32,256]{3,2,1,0:T(8,128)(2,1)S(1)}, u32[]{:S(2)}, u32[]{:S(2)}) collective-permute-start(bf16[2,2,32,256]{3,2,1,0:T(8,128)(2,1)S(1)} %bitcast.15), channel_id=1, source_target_pairs={{0,2},{1,9},{2,0},{3,11},{4,6},{5,13},{6,4},{7,15},{8,10},{9,1},{1... | collective-permute-start | bytes 196616 | tf_op jit(solution)/shard_map/ppermute | solution.py:196
  6.2 6.4 %collective-permute-start.1 = (bf16[3,2,32,256]{3,2,1,0:T(8,128)(2,1)S(1)}, bf16[3,2,32,256]{3,2,1,0:T(8,128)(2,1)S(1)}, u32[]{:S(2)}, u32[]{:S(2)}) collective-permute-start(bf16[3,2,32,256]{3,2,1,0:T(8,128)(2,1)S(1)} %pad_maximum_fusion.outer), channel_id=1, source_target_pairs={{0,8},{1,5},{2,10},{3,7},{4,12},{5,1},{6,14},{7,3},{8,0},{9,13},{1... | collective-permute-start | bytes 294920 | tf_op jit(solution)/shard_map/ppermute | solution.py:196
  11.0 8.5 %collective-permute-start.3 = (bf16[6,2,32,256]{3,2,1,0:T(8,128)(2,1)S(1)}, bf16[6,2,32,256]{3,2,1,0:T(8,128)(2,1)S(1)}, u32[]{:S(2)}, u32[]{:S(2)}) collective-permute-start(bf16[6,2,32,256]{3,2,1,0:T(8,128)(2,1)S(1)} %get-tuple-element.11.own), channel_id=1, source_target_pairs={{0,2},{2,4},{4,6},{6,8},{8,10},{10,12},{12,14},{14,0},{1,3},{3,5},... | collective-permute-start | bytes 589832 | tf_op jit(solution)/shard_map/ppermute | solution.py:254
  12.6 6.9 %collective-permute-start.2 = (bf16[3,2,32,256]{3,2,1,0:T(8,128)(2,1)S(1)}, bf16[3,2,32,256]{3,2,1,0:T(8,128)(2,1)S(1)}, u32[]{:S(2)}, u32[]{:S(2)}) collective-permute-start(bf16[3,2,32,256]{3,2,1,0:T(8,128)(2,1)S(1)} %pad_maximum_fusion.1.inner), channel_id=1, source_target_pairs={{0,4},{1,3},{2,6},{3,1},{4,0},{5,7},{6,2},{7,5},{8,12},{9,11},{10,... | collective-permute-start | bytes 294920 | tf_op jit(solution)/shard_map/ppermute | solution.py:196
  14.3 4.3 %collective-permute-start.4 = (bf16[2,2,32,256]{3,2,1,0:T(8,128)(2,1)S(1)}, bf16[2,2,32,256]{3,2,1,0:T(8,128)(2,1)S(1)}, u32[]{:S(2)}, u32[]{:S(2)}) collective-permute-start(bf16[2,2,32,256]{3,2,1,0:T(8,128)(2,1)S(1)} %slice.39), channel_id=1, source_target_pairs={{0,4},{1,3},{2,6},{3,1},{4,0},{5,7},{6,2},{7,5},{8,12},{9,11},{10,... | collective-permute-start | bytes 196616 | tf_op jit(solution)/shard_map/ppermute | solution.py:196

commit v2 on v1

--- a/solution.py
+++ b/solution.py
@@ -27,6 +27,18 @@
     here = lax.broadcasted_iota(jnp.int32, (n, n), 0)
     there = lax.broadcasted_iota(jnp.int32, (n, n), 1)
     return jnp.sum(jnp.where(here == there, row, 0), axis=1, keepdims=True)
+
+
+def pack_kernel(*refs):
+    sources, packed, sems = refs[:-2], refs[-2], refs[-1]
+    copies = [
+        pltpu.make_async_copy(src, packed.at[i // 2, i % 2], sems.at[i])
+        for i, src in enumerate(sources)
+    ]
+    for copy in copies:
+        copy.start()
+    for copy in copies:
+        copy.wait()
 
 
 def blend_kernel(*refs):
@@ -222,12 +234,20 @@
     vm = pl.BlockSpec(memory_space=pltpu.VMEM)
     sm = pl.BlockSpec(memory_space=pltpu.SMEM)
 
-    packed = jnp.stack(
-        [
-            a.reshape(block, width)
-            for a in (prefix_key_cache, prefix_value_cache, completed_keys, completed_values)
-        ]
-    ).reshape(2, 2, block, width)
+    hbm = pl.BlockSpec(memory_space=pltpu.HBM)
+    blocks = [
+        a.reshape(block, width)
+        for a in (prefix_key_cache, prefix_value_cache, completed_keys, completed_values)
+    ]
+    packed = pl.pallas_call(
+        pack_kernel,
+        out_shape=pltpu.VMEM((2, 2, block, width), jnp.bfloat16),
+        in_specs=[hbm] * len(blocks),
+        out_specs=vm,
+        scratch_shapes=[pltpu.SemaphoreType.DMA((len(blocks),))],
+        compiler_params=pltpu.CompilerParams(vmem_limit_bytes=4 << 20),
+        name="pack",
+    )(*(pltpu.with_memory_space_constraint(a, pltpu.HBM) for a in blocks))
 
     sources = (
         rounds,

time: 21.4 us -> 21.4 us (level)
  Pallas kernels: 4.1 us -> 4.96 us
  other arithmetic: 0.89 us -> 0.05 us
    pallas_call x0 -> x1, Pallas kernels: none -> 0.87 us  [on_device(): pl.pallas_call(pack_kernel, out_shape=pltpu.VMEM((2, 2, block, width), jn...]
    another operation x1 -> x0, other arithmetic: 0.84 us -> none  [on_device(): jnp.stack([a.reshape(block, width) for a in (prefix_key_cache, prefix_val...]
where the time goes in v2:
time: 21.4 us; the launch traced here: 21.1 us
  starting transfers between devices  9.85 us (46%)
  waiting for transfers between devices  5.49 us (26%)
  Pallas kernels  4.96 us (23%)
  between operations  0.72 us (3%)
    ppermute x4, starting transfers between devices, swap(): return lax.ppermute(block, ('blk', 'mp'), pairs)  8.31 us
    ppermute x4, waiting for transfers between devices, swap(): return lax.ppermute(block, ('blk', 'mp'), pairs)  5.41 us
    pallas_call x1, Pallas kernels, on_device(): pl.pallas_call(blend_kernel, out_shape=[pltpu.VMEM((slots, 2, block, widt...  1.68 us
    ppermute x1, starting transfers between devices, on_device(): prev = lax.ppermute(own, 'blk', [(i, (i + 1) % size) for i in range(size)])  1.54 us
    pallas_call x1, Pallas kernels, on_device(): pl.pallas_call(last_kernel, out_shape=jax.ShapeDtypeStruct((slots, block,...  1.5 us
    pallas_call x1, Pallas kernels, on_device(): pl.pallas_call(first_kernel, out_shape=shapes, in_specs=[sm] + [vm] * 5,...  0.92 us
    pallas_call x1, Pallas kernels, on_device(): pl.pallas_call(pack_kernel, out_shape=pltpu.VMEM((2, 2, block, width), jn...  0.87 us
  transfers between devices with their start and end apart: 5, of which 3 were waited for; matrix products, arithmetic and copies ran while one was open for 0% of the time, Pallas kernels for 12%

profile of v2, /device:TPU:0, one launch (start us, length us, event | category | flops | bytes accessed | tf_op | source)
XLA Modules:
  0.0 21.1 jit_solution(9206197807527572849)
XLA Ops:
  0.0 0.0 copy-start
  0.0 0.9 %pack.1 = bf16[2,2,32,256]{3,2,1,0:T(8,128)(2,1)S(1)} custom-call(bf16[32,256]{1,0:T(8,128)(2,1)} %bitcast.16, bf16[32,256]{1,0:T(8,128)(2,1)} %bitcast.17, bf16[32,256]{1,0:T(8,128)(2,1)} %bitcast.18, bf16[32,256]{1,0:T(8,128)(2,1)} %bitcast.19), custom_call_target="tpu_custom_call" | custom-call | tf_op jit(solution)/shard_map/pack/pallas_call | solution.py:242
  0.9 3.0 %collective-permute-start = (bf16[2,2,32,256]{3,2,1,0:T(8,128)(2,1)S(1)}, bf16[2,2,32,256]{3,2,1,0:T(8,128)(2,1)S(1)}, u32[]{:S(2)}, u32[]{:S(2)}) collective-permute-start(bf16[2,2,32,256]{3,2,1,0:T(8,128)(2,1)S(1)} %pack.1), channel_id=1, source_target_pairs={{0,2},{1,9},{2,0},{3,11},{4,6},{5,13},{6,4},{7,15},{8,10},{9,1},{1... | collective-permute-start | bytes 196616 | tf_op jit(solution)/shard_map/ppermute | solution.py:208
  4.6 1.6 %collective-permute-done = bf16[2,2,32,256]{3,2,1,0:T(8,128)(2,1)S(1)} collective-permute-done((bf16[2,2,32,256]{3,2,1,0:T(8,128)(2,1)S(1)}, bf16[2,2,32,256]{3,2,1,0:T(8,128)(2,1)S(1)}, u32[]{:S(2)}, u32[]{:S(2)}) %collective-permute-start) | collective-permute-done | bytes 65568 | tf_op jit(solution)/shard_map/ppermute | solution.py:208
  6.2 3.2 %collective-permute-start.1 = (bf16[3,2,32,256]{3,2,1,0:T(8,128)(2,1)S(1)}, bf16[3,2,32,256]{3,2,1,0:T(8,128)(2,1)S(1)}, u32[]{:S(2)}, u32[]{:S(2)}) collective-permute-start(bf16[3,2,32,256]{3,2,1,0:T(8,128)(2,1)S(1)} %pad_maximum_fusion.outer), channel_id=1, source_target_pairs={{0,8},{1,5},{2,10},{3,7},{4,12},{5,1},{6,14},{7,3},{8,0},{9,13},{1... | collective-permute-start | bytes 294920 | tf_op jit(solution)/shard_map/ppermute | solution.py:208
  9.4 1.7 %blend.1 = (bf16[6,2,32,256]{3,2,1,0:T(8,128)(2,1)S(1)}, f32[6,1,256]{2,1,0:T(1,128)S(1)}) custom-call(s32[1,6]{1,0:T(1,128)} %bitcast.20, s32[6,1,32]{2,1,0:T(1,128)} %refs_1_.1, s32[6,1,32]{2,1,0:T(1,128)} %refs_2_.1, bf16[64,256]{1,0:T(8,128)(2,1)} %refs_3_.1, bf16[64,256]{1,0:T(8,128)(2,1)} %refs_4_.1, bf16[6,1,32,256]{3,2,1,0:T(8,128)(2,1)} %refs_5_.1, ...), custom_call_target="tpu_custom_call" | custom-call | tf_op jit(solution)/shard_map/blend/pallas_call | solution.py:261
  11.1 1.5 %collective-permute-start.3 = (bf16[6,2,32,256]{3,2,1,0:T(8,128)(2,1)S(1)}, bf16[6,2,32,256]{3,2,1,0:T(8,128)(2,1)S(1)}, u32[]{:S(2)}, u32[]{:S(2)}) collective-permute-start(bf16[6,2,32,256]{3,2,1,0:T(8,128)(2,1)S(1)} %get-tuple-element.11.own), channel_id=1, source_target_pairs={{0,2},{2,4},{4,6},{6,8},{8,10},{10,12},{12,14},{14,0},{1,3},{3,5},... | collective-permute-start | bytes 589832 | tf_op jit(solution)/shard_map/ppermute | solution.py:274
  12.6 0.0 collective-permute-done.1
  12.7 1.6 %collective-permute-start.2 = (bf16[3,2,32,256]{3,2,1,0:T(8,128)(2,1)S(1)}, bf16[3,2,32,256]{3,2,1,0:T(8,128)(2,1)S(1)}, u32[]{:S(2)}, u32[]{:S(2)}) collective-permute-start(bf16[3,2,32,256]{3,2,1,0:T(8,128)(2,1)S(1)} %pad_maximum_fusion.1.inner), channel_id=1, source_target_pairs={{0,4},{1,3},{2,6},{3,1},{4,0},{5,7},{6,2},{7,5},{8,12},{9,11},{10,... | collective-permute-start | bytes 294920 | tf_op jit(solution)/shard_map/ppermute | solution.py:208
  14.3 0.4 %collective-permute-start.4 = (bf16[2,2,32,256]{3,2,1,0:T(8,128)(2,1)S(1)}, bf16[2,2,32,256]{3,2,1,0:T(8,128)(2,1)S(1)}, u32[]{:S(2)}, u32[]{:S(2)}) collective-permute-start(bf16[2,2,32,256]{3,2,1,0:T(8,128)(2,1)S(1)} %slice.39), channel_id=1, source_target_pairs={{0,4},{1,3},{2,6},{3,1},{4,0},{5,7},{6,2},{7,5},{8,12},{9,11},{10,... | collective-permute-start | bytes 196616 | tf_op jit(solution)/shard_map/ppermute | solution.py:208
  14.8 3.8 %collective-permute-done.4.side = bf16[2,2,32,256]{3,2,1,0:T(8,128)(2,1)S(1)} collective-permute-done((bf16[2,2,32,256]{3,2,1,0:T(8,128)(2,1)S(1)}, bf16[2,2,32,256]{3,2,1,0:T(8,128)(2,1)S(1)}, u32[]{:S(2)}, u32[]{:S(2)}) %collective-permute-start.4) | collective-permute-done | bytes 65568 | tf_op jit(solution)/shard_map/ppermute | solution.py:208
  18.6 0.0 copy-done
  18.6 0.9 %early.1 = (f32[6,2,1,256]{3,2,1,0:T(1,128)S(1)}, f32[6,2,1,256]{3,2,1,0:T(1,128)S(1)}, f32[6,2,128,256]{3,2,1,0:T(8,128)S(1)}, s32[8,128]{1,0:T(8,128)S(1)}) custom-call(s32[1]{0:T(128)} %bitcast.7.took, bf16[6,32,1792]{2,1,0:T(8,128)(2,1)S(1)} %bitcast.14, bf16[3,2,32,256]{3,2,1,0:T(8,128)(2,1)S(1)} %pad_maximum_fusion.outer, ...), custom_call_target="tpu_custom_call" | custom-call | tf_op jit(solution)/shard_map/early/pallas_call | solution.py:298
  19.5 0.1 collective-permute-done.3.prev
  19.6 0.0 collective-permute-done.2.far
  19.6 1.5 %late.1 = bf16[6,32,1792]{2,1,0:T(8,128)(2,1)} custom-call(bf16[6,32,1792]{2,1,0:T(8,128)(2,1)S(1)} %bitcast.15, bf16[3,2,32,256]{3,2,1,0:T(8,128)(2,1)S(1)} %pad_maximum_fusion.1.inner, bf16[3,2,32,256]{3,2,1,0:T(8,128)(2,1)S(1)} %collective-permute-done.2.far, bf16[6,2,32,256]{3,2,1,0:T(8,128)(2,1)S(1)} %collective-permute-done.3.prev, ...), custom_call_target="tpu_custom_call" | custom-call | tf_op jit(solution)/shard_map/late/pallas_call | solution.py:306
  (6 shorter events, 0.1 us)
Async XLA Ops:
  0.0 18.6 %copy-start = (bf16[6,1,32,1792]{3,2,1,0:T(8,128)(2,1)S(1)}, bf16[6,1,32,1792]{3,2,1,0:T(8,128)(2,1)}, u32[]{:S(2)}) copy-start(bf16[6,1,32,1792]{3,2,1,0:T(8,128)(2,1)} %param.13) | copy-start | bytes 2064388
  0.9 5.3 %collective-permute-start = (bf16[2,2,32,256]{3,2,1,0:T(8,128)(2,1)S(1)}, bf16[2,2,32,256]{3,2,1,0:T(8,128)(2,1)S(1)}, u32[]{:S(2)}, u32[]{:S(2)}) collective-permute-start(bf16[2,2,32,256]{3,2,1,0:T(8,128)(2,1)S(1)} %pack.1), channel_id=1, source_target_pairs={{0,2},{1,9},{2,0},{3,11},{4,6},{5,13},{6,4},{7,15},{8,10},{9,1},{1... | collective-permute-start | bytes 196616 | tf_op jit(solution)/shard_map/ppermute | solution.py:208
  6.2 6.4 %collective-permute-start.1 = (bf16[3,2,32,256]{3,2,1,0:T(8,128)(2,1)S(1)}, bf16[3,2,32,256]{3,2,1,0:T(8,128)(2,1)S(1)}, u32[]{:S(2)}, u32[]{:S(2)}) collective-permute-start(bf16[3,2,32,256]{3,2,1,0:T(8,128)(2,1)S(1)} %pad_maximum_fusion.outer), channel_id=1, source_target_pairs={{0,8},{1,5},{2,10},{3,7},{4,12},{5,1},{6,14},{7,3},{8,0},{9,13},{1... | collective-permute-start | bytes 294920 | tf_op jit(solution)/shard_map/ppermute | solution.py:208
  11.1 8.5 %collective-permute-start.3 = (bf16[6,2,32,256]{3,2,1,0:T(8,128)(2,1)S(1)}, bf16[6,2,32,256]{3,2,1,0:T(8,128)(2,1)S(1)}, u32[]{:S(2)}, u32[]{:S(2)}) collective-permute-start(bf16[6,2,32,256]{3,2,1,0:T(8,128)(2,1)S(1)} %get-tuple-element.11.own), channel_id=1, source_target_pairs={{0,2},{2,4},{4,6},{6,8},{8,10},{10,12},{12,14},{14,0},{1,3},{3,5},... | collective-permute-start | bytes 589832 | tf_op jit(solution)/shard_map/ppermute | solution.py:274
  12.7 6.9 %collective-permute-start.2 = (bf16[3,2,32,256]{3,2,1,0:T(8,128)(2,1)S(1)}, bf16[3,2,32,256]{3,2,1,0:T(8,128)(2,1)S(1)}, u32[]{:S(2)}, u32[]{:S(2)}) collective-permute-start(bf16[3,2,32,256]{3,2,1,0:T(8,128)(2,1)S(1)} %pad_maximum_fusion.1.inner), channel_id=1, source_target_pairs={{0,4},{1,3},{2,6},{3,1},{4,0},{5,7},{6,2},{7,5},{8,12},{9,11},{10,... | collective-permute-start | bytes 294920 | tf_op jit(solution)/shard_map/ppermute | solution.py:208
  14.3 4.3 %collective-permute-start.4 = (bf16[2,2,32,256]{3,2,1,0:T(8,128)(2,1)S(1)}, bf16[2,2,32,256]{3,2,1,0:T(8,128)(2,1)S(1)}, u32[]{:S(2)}, u32[]{:S(2)}) collective-permute-start(bf16[2,2,32,256]{3,2,1,0:T(8,128)(2,1)S(1)} %slice.39), channel_id=1, source_target_pairs={{0,4},{1,3},{2,6},{3,1},{4,0},{5,7},{6,2},{7,5},{8,12},{9,11},{10,... | collective-permute-start | bytes 196616 | tf_op jit(solution)/shard_map/ppermute | solution.py:208
